TPU v7x, 256 devices: a whole 4x4x8 slice. The times are simulated.
256 devices in a mesh: period: 128 (over z, x, y), half: 2 (over core).
Axes of the slice: x: 4, y: 4, z: 8, core: 2. Of those that a mesh axis runs over, the one named last changes fastest.
Arguments:
- probes: float32 [1024, 4, 512], P('period', None, 'half'), may hold values from -6 to 6
- footprints: bfloat16 [1024, 512, 512], P('period', None, 'half'), may hold values from -0.25 to 0.25
- lag_weights: float32 [1024, 4], P('period'), may hold values from 0.2 to 2
- owners: int32 [1024, 4], P('period'), may hold values from 0 to 127, all different within a row; in each aligned block of 8 rows (0 to 7, 8 to 15, ...) at most 2 rows name the same one
- window_tiles: int32 [1024, 2], P('period', 'half'), may hold values from 0 to 10
- coords: int32 [2, 3072], replicated, may hold values from 0 to 63
- temporal: float32 [128, 128], replicated, as said below
Outputs:
- coefficients: float32 [4, 4], replicated
- residual: float32 [1024, 4, 512], P('period', None, 'half')
Inputs may be any that keep to these rules, and one draw needn't show every extreme that they name: `owners`: each row names 4 different periods. Among the 8 rows of one index of period, no period is named more than 2 times, and one is named exactly 2 times. `temporal`: symmetric.
All inputs are finite; a program needn't handle non-finite values.
Results may differ from a plain program's by a relative error of at most 0.025.
Values may be sent and summed in bfloat16 or wider, within the bound.
No kernel may reach another device: no remote copies, remote signals or barrier semaphores. Data moves between devices by JAX's collectives and lax.ppermute only.
A program may use at most 64 MiB of HBM per device.

v0:
```python
import jax
import jax.numpy as jnp
from jax import lax
from jax.sharding import PartitionSpec as P

epsilon = 1e-06
kernel_scale = 0.05
kernel_length = 6.0
highest = lax.Precision.HIGHEST


def from_partner(block, axis, bit):
    count = lax.axis_size(axis)
    route = []
    for low in range(count):
        high = low | 1 << bit
        if high != low and high < count:
            route += [(low, high), (high, low)]
    return lax.ppermute(block, axis, route)


def body(probes, footprints, lag_weights, owners, window_tiles, coords, temporal):
    periods = lax.axis_size("period")
    half_index = lax.axis_index("half")
    block_count, top_count = owners.shape
    probe_count = probes.shape[1]
    sound_count = footprints.shape[1]
    window = footprints.shape[2]
    win_tiles = window // 128
    cell_count = coords.shape[1]
    half_cells = cell_count // 2
    tile_count = half_cells // 128
    group_cells = half_cells // periods
    total_rows = float(block_count * periods * sound_count)
    tiles = window_tiles[:, 0]
    tile_hot = (
        tiles[:, None, None] + jnp.arange(win_tiles, dtype=jnp.int32)[None, :, None]
        == jnp.arange(tile_count, dtype=jnp.int32)[None, None, :]
    ).astype(jnp.float32)
    own_coords = lax.dynamic_slice_in_dim(coords, half_index * half_cells, half_cells, 1)
    delta_x = own_coords[0][:, None] - coords[0][None, :]
    delta_y = own_coords[1][:, None] - coords[1][None, :]
    squared = (delta_x * delta_x + delta_y * delta_y).astype(jnp.float32)
    kernel_rows = (kernel_scale * jnp.exp(-jnp.sqrt(squared) / kernel_length)).reshape(
        periods, group_cells, cell_count
    )
    owner_hot = (owners[:, :, None] == jnp.arange(periods, dtype=jnp.int32)[None, None, :]).astype(
        jnp.float32
    )

    def add_half(piece_rows):
        return jnp.einsum(
            "bps,bsw->bpw", piece_rows, footprints, preferred_element_type=jnp.float32
        )

    def mix_periods(grouped_part):
        mixed_part = jnp.einsum("ts,sik->tik", temporal, grouped_part, precision=highest)
        return lax.all_to_all(mixed_part, "period", split_axis=0, concat_axis=0, tiled=True)

    def apply_operator(vector):
        vector_low = vector.astype(jnp.bfloat16)
        partial_value = add_half(lax.all_gather(vector_low, "half", axis=2, tiled=True))
        terms = lag_weights[:, :, None, None] * partial_value[:, None, :, :]
        term_tiles = terms.reshape(block_count, top_count, probe_count, win_tiles, 128)
        placed = jnp.einsum("bjt,bkpjl->bkptl", tile_hot, term_tiles, precision=highest)
        dense_terms = jnp.einsum("bkn,bkptl->nptl", owner_hot, placed, precision=highest)
        summed = lax.psum_scatter(
            dense_terms.reshape(periods, probe_count, half_cells),
            "period",
            scatter_dimension=0,
            tiled=True,
        )
        flux_half = summed[0]
        other_half = from_partner(flux_half, "half", 0)
        whole_flux = jnp.where(
            half_index == 0,
            jnp.concatenate([flux_half, other_half], axis=1),
            jnp.concatenate([other_half, flux_half], axis=1),
        )
        grouped = jnp.einsum("pc,gkc->gpk", whole_flux, kernel_rows, precision=highest)
        mixed_flux = mix_periods(
            lax.all_to_all(grouped, "period", split_axis=0, concat_axis=0, tiled=True)
        )
        field_low = (
            jnp.transpose(mixed_flux, (1, 0, 2))
            .reshape(probe_count, half_cells)
            .astype(jnp.bfloat16)
        )
        field_all = lax.all_gather(field_low[None], "period", axis=0, tiled=True)
        selected = jnp.einsum(
            "bkn,npc->bkpc",
            owner_hot.astype(jnp.bfloat16),
            field_all,
            preferred_element_type=jnp.float32,
        )
        selected = selected.reshape(block_count, top_count, probe_count, tile_count, 128)
        windows = jnp.einsum("bkptl,bjt->bkpjl", selected, tile_hot, precision=highest)
        windows = windows.astype(jnp.bfloat16).reshape(block_count, top_count, probe_count, window)
        products = jnp.einsum(
            "bkpw,bsw->bkps", windows, footprints, preferred_element_type=jnp.float32
        )
        sounded = jnp.einsum("bk,bkps->bps", lag_weights, products, precision=highest)
        return lax.psum_scatter(
            sounded.astype(jnp.bfloat16), "half", scatter_dimension=2, tiled=True
        ).astype(jnp.float32)

    def local_mean(values):
        return jnp.sum(values, axis=(0, 2))

    def lanczos_step(current, image):
        inner_sum = lax.psum(local_mean(current * image), ("period", "half"))
        alpha = inner_sum / total_rows
        remainder = image - alpha[None, :, None] * current
        square_sum = lax.psum(local_mean(remainder * remainder), ("period", "half"))
        beta = jnp.sqrt(square_sum / total_rows + epsilon)
        return (alpha, remainder, beta)

    start_sum = lax.psum(local_mean(probes * probes), ("period", "half"))
    first_q = probes / jnp.sqrt(start_sum / total_rows + epsilon)[None, :, None]
    image_one = apply_operator(first_q)
    alpha_one, rest_one, beta_one = lanczos_step(first_q, image_one)
    second_q = rest_one / beta_one[None, :, None]
    image_two = apply_operator(second_q) - beta_one[None, :, None] * first_q
    alpha_two, residual, beta_two = lanczos_step(second_q, image_two)
    coefficients = jnp.stack([alpha_one, beta_one, alpha_two, beta_two], axis=0)
    return (coefficients, residual)


def solution(mesh):
    in_specs = (
        P("period", None, "half"),
        P("period", None, "half"),
        P("period", None),
        P("period", None),
        P("period", "half"),
        P(),
        P(),
    )
    out_specs = (P(), P("period", None, "half"))
    return jax.shard_map(body, mesh=mesh, in_specs=in_specs, out_specs=out_specs, check_vma=False)
```

profile of v0, /device:TPU:1, one launch (start us, length us, event | category | flops | bytes accessed | tf_op | source)
XLA Modules:
  0.0 1305.8 jit_solution(13119377155676004425)
XLA Ops:
  7.2 1.0 multiply_reduce_fusion.3
  8.3 81.4 %psum.35 = f32[4]{0:T(128)S(1)} all-reduce(f32[4]{0:T(128)S(1)} %multiply_reduce_fusion.3), channel_id=1, replica_groups=mesh['period'=128,'half'=2] {'period','half'}, use_global_device_ids=true, to_apply=%region_1.0 | all-reduce | flops 4 | bytes 32 | tf_op jit(solution)/shard_map/psum | solution.py:118
  89.7 0.7 iota_add_fusion
  90.4 0.8 copy.24
  91.2 0.8 fusion.101
  92.0 2.5 all_gather.12
  94.9 0.8 convolution_bitcast_fusion.1
  95.7 4.4 fusion.38
  100.1 5.1 copy.26
  106.4 221.5 %all-reduce.5.cloned.1.call-done = f32[128,4,1536]{2,1,0:T(4,128)} async-done(((f32[128,4,1536]{2,1,0:T(4,128)}), f32[128,4,1536]{2,1,0:T(4,128)}) %all-reduce.5.cloned.1.call-update) | async-done | bytes 3145744
  328.0 1.4 dynamic-slice_bitcast_fusion.1
  329.4 4.9 collective-permute-start
  335.2 46.6 %fusion.32 = f32[128,4,12]{0,1,2:T(4,128)S(1)} fusion(s32[3072]{0:T(1024)S(1)} %bitcast.132, s32[128,12]{0,1:T(8,128)S(1)} %copy.23, s32[3072]{0:T(1024)S(1)} %bitcast.130, s32[128,12]{0,1:T(8,128)S(1)} %copy.22, f32[4,1536]{1,0:T(4,128)S(1)} %collective-permute-done, f32[4,1536]{1,0:T(4,128)S(1)} %dynamic-slice_bitcast_fusion.1, pred[]{:T(512)S(6)} %eq.36), kind=kOutput, calls=%fused_computation.35 | convolution fusion | flops 268996608 | bytes 110593 | tf_op jit(solution)/shard_map/pc,gkc->gpk/dot_general | solution.py:80
  382.0 23.7 %all_to_all.20 = f32[128,4,12]{2,1,0:T(4,128)S(1)} all-to-all(f32[128,4,12]{2,1,0:T(4,128)S(1)} %copy.27), channel_id=1, replica_groups=mesh['period'=128,'half'=2] {'period'}, dimensions={0} | all-to-all | bytes 49152 | tf_op jit(solution)/shard_map/all_to_all | solution.py:82
  406.4 17.2 %all_to_all.21 = bf16[128,4,12]{2,1,0:T(4,128)(2,1)S(1)} all-to-all(bf16[128,4,12]{2,1,0:T(4,128)(2,1)S(1)} %copy.29), channel_id=1, replica_groups=mesh['period'=128,'half'=2] {'period'}, dimensions={0} | all-to-all | bytes 24576 | tf_op jit(solution)/shard_map/all_to_all | solution.py:58
  423.7 0.8 convert_element_type.80
  424.8 94.2 %all-gather.3.cloned.1.call-done = bf16[128,4,1536]{2,1,0:T(4,128)(2,1)} async-done(((bf16[1,4,1536]{2,1,0:T(4,128)(2,1)}), bf16[128,4,1536]{2,1,0:T(4,128)(2,1)}) %all-gather.3.cloned.1.call-update) | async-done | bytes 1572880 | tf_op jit(solution)/shard_map/all_gather | solution.py:89
  519.0 2.0 fusion.24
  521.7 0.6 fusion.16
  522.3 0.6 fusion.42
  523.0 0.7 copy.52
  523.7 1.3 reshape.130
  525.1 16.9 %reduce-scatter.7.cloned.1.call-done = bf16[256,32]{1,0:T(8,128)(2,1)} async-done(((bf16[512,32]{1,0:T(8,128)(2,1)}), bf16[256,32]{1,0:T(8,128)(2,1)}) %reduce-scatter.7.cloned.1.call-update) | async-done | bytes 16400
  542.0 1.2 reshape.131
  543.7 77.4 %psum.36 = f32[4]{0:T(128)S(1)} all-reduce(f32[4]{0:T(128)S(1)} %fusion.68), channel_id=1, replica_groups=mesh['period'=128,'half'=2] {'period','half'}, use_global_device_ids=true, to_apply=%region_5.6 | all-reduce | flops 4 | bytes 32 | tf_op jit(solution)/shard_map/psum | solution.py:111
  621.3 73.1 %psum.37 = f32[4]{0:T(128)S(1)} all-reduce(f32[4]{0:T(128)S(1)} %multiply_reduce_fusion.2), channel_id=1, replica_groups=mesh['period'=128,'half'=2] {'period','half'}, use_global_device_ids=true, to_apply=%region_7.8 | all-reduce | flops 4 | bytes 32 | tf_op jit(solution)/shard_map/psum | solution.py:114
  694.5 2.2 all_gather.14
  697.1 0.8 convolution_bitcast_fusion
  697.9 4.4 fusion.36
  702.3 5.1 copy.34
  707.5 223.8 %all-reduce.7.cloned.1.call-done = f32[128,4,1536]{2,1,0:T(4,128)} async-done(((f32[128,4,1536]{2,1,0:T(4,128)}), f32[128,4,1536]{2,1,0:T(4,128)}) %all-reduce.7.cloned.1.call-update) | async-done | bytes 3145744
  931.3 1.4 dynamic-slice_bitcast_fusion
  932.7 4.9 collective-permute-start.1
  937.6 0.8 collective-permute-done.1
  938.5 46.6 %fusion.33 = f32[128,4,12]{0,1,2:T(4,128)S(1)} fusion(s32[3072]{0:T(1024)S(1)} %bitcast.133, s32[128,12]{0,1:T(8,128)S(1)} %copy.23, s32[3072]{0:T(1024)S(1)} %bitcast.131, s32[128,12]{0,1:T(8,128)S(1)} %copy.22, f32[4,1536]{1,0:T(4,128)S(1)} %collective-permute-done.1, f32[4,1536]{1,0:T(4,128)S(1)} %dynamic-slice_bitcast_fusion, pred[]{:T(512)S(6)} %eq.36), kind=kOutput, calls=%fused_computation.36 | convolution fusion | flops 268996608 | bytes 110593 | tf_op jit(solution)/shard_map/pc,gkc->gpk/dot_general | solution.py:80
  985.3 23.7 %all_to_all.22 = f32[128,4,12]{2,1,0:T(4,128)S(1)} all-to-all(f32[128,4,12]{2,1,0:T(4,128)S(1)} %copy.35), channel_id=1, replica_groups=mesh['period'=128,'half'=2] {'period'}, dimensions={0} | all-to-all | bytes 49152 | tf_op jit(solution)/shard_map/all_to_all | solution.py:82
  1009.7 17.2 %all_to_all.23 = bf16[128,4,12]{2,1,0:T(4,128)(2,1)S(1)} all-to-all(bf16[128,4,12]{2,1,0:T(4,128)(2,1)S(1)} %copy.37), channel_id=1, replica_groups=mesh['period'=128,'half'=2] {'period'}, dimensions={0} | all-to-all | bytes 24576 | tf_op jit(solution)/shard_map/all_to_all | solution.py:58
  1027.0 0.8 convert_element_type.88
  1027.9 94.5 %all-gather.5.cloned.1.call-done = bf16[128,4,1536]{2,1,0:T(4,128)(2,1)} async-done(((bf16[1,4,1536]{2,1,0:T(4,128)(2,1)}), bf16[128,4,1536]{2,1,0:T(4,128)(2,1)}) %all-gather.5.cloned.1.call-update) | async-done | bytes 1572880 | tf_op jit(solution)/shard_map/all_gather | solution.py:89
  1122.3 2.0 fusion.27
  1125.0 0.6 fusion.14
  1126.3 0.7 copy.54
  1127.0 1.3 reshape.132
  1128.4 16.9 %reduce-scatter.9.cloned.1.call-done = bf16[256,32]{1,0:T(8,128)(2,1)} async-done(((bf16[512,32]{1,0:T(8,128)(2,1)}), bf16[256,32]{1,0:T(8,128)(2,1)}) %reduce-scatter.9.cloned.1.call-update) | async-done | bytes 16400
  1145.3 1.2 reshape.133
  1147.0 77.4 %psum.38 = f32[4]{0:T(128)S(1)} all-reduce(f32[4]{0:T(128)S(1)} %multiply_reduce_fusion.1), channel_id=1, replica_groups=mesh['period'=128,'half'=2] {'period','half'}, use_global_device_ids=true, to_apply=%region_11.12 | all-reduce | flops 4 | bytes 32 | tf_op jit(solution)/shard_map/psum | solution.py:111
  1224.5 0.8 multiply_reduce_fusion
  1225.3 73.1 %psum.39 = f32[4]{0:T(128)S(1)} all-reduce(f32[4]{0:T(128)S(1)} %get-tuple-element.4), channel_id=1, replica_groups=mesh['period'=128,'half'=2] {'period','half'}, use_global_device_ids=true, to_apply=%region_13.14 | all-reduce | flops 4 | bytes 32 | tf_op jit(solution)/shard_map/psum | solution.py:114
  (64 shorter events, 9.1 us)
Async XLA Ops:
  7.2 87.3 %copy-start = (bf16[8,512,256]{2,1,0:T(8,128)(2,1)S(1)}, bf16[8,512,256]{2,1,0:T(8,128)(2,1)}, u32[]{:S(2)}) copy-start(bf16[8,512,256]{2,1,0:T(8,128)(2,1)} %param.8) | copy-start | bytes 6291460
  7.2 88.5 %copy-start.3 = (s32[8,4]{0,1:T(4,128)S(1)}, s32[8,4]{0,1:T(4,128)}, u32[]{:S(2)}) copy-start(s32[8,4]{0,1:T(4,128)} %param.10) | copy-start | bytes 388
  7.2 320.8 %all-reduce.5.cloned.1.call-start = ((), (), s32[]{:S(2)}) async-start(), calls=%async_computation.10 | async-start | bytes 6291456
  105.2 0.7 copy-start.5
  105.2 229.1 %copy-start.2 = (s32[2,3072]{1,0:T(2,128)S(1)}, s32[2,3072]{1,0:T(2,128)}, u32[]{:S(2)}) copy-start(s32[2,3072]{1,0:T(2,128)} %param.12) | copy-start | bytes 73732
  105.2 413.8 %all-gather.3.cloned.1.call-start = ((), (), s32[]{:S(2)}) async-start(), calls=%async_computation.6 | async-start | bytes 1585152 | tf_op jit(solution)/shard_map/all_gather | solution.py:89
  329.4 5.8 collective-permute-start
  335.2 70.5 %copy-start.1 = (f32[128,128]{1,0:T(8,128)S(1)}, f32[128,128]{1,0:T(8,128)}, u32[]{:S(2)}) copy-start(f32[128,128]{1,0:T(8,128)} %param.13) | copy-start | bytes 196612
  335.2 89.6 %copy-start.4 = (f32[8,4]{0,1:T(4,128)S(1)}, f32[8,4]{0,1:T(4,128)}, u32[]{:S(2)}) copy-start(f32[8,4]{0,1:T(4,128)} %param.9) | copy-start | bytes 388
  424.5 117.5 %reduce-scatter.7.cloned.1.call-start = ((), (), s32[]{:S(2)}) async-start(), calls=%async_computation.8 | async-start | bytes 196608
  525.0 406.2 %all-reduce.7.cloned.1.call-start = ((), (), s32[]{:S(2)}) async-start(), calls=%async_computation.11 | async-start | bytes 6291456
  707.4 414.9 %all-gather.5.cloned.1.call-start = ((), (), s32[]{:S(2)}) async-start(), calls=%async_computation.7 | async-start | bytes 1585152 | tf_op jit(solution)/shard_map/all_gather | solution.py:89
  932.7 5.8 collective-permute-start.1
  1027.8 117.5 %reduce-scatter.9.cloned.1.call-start = ((), (), s32[]{:S(2)}) async-start(), calls=%async_computation.9 | async-start | bytes 196608
Sparse Core Ops, SparseCore 0:
  105.3 222.5 all-reduce.4
  424.6 94.3 all-gather.2
  525.2 16.7 reduce-scatter.6
  707.5 223.6 all-reduce.6
  1027.9 94.3 all-gather.4
  1128.5 16.7 reduce-scatter.8
where the time goes:
time: 1310 us
  waiting for transfers between devices  669 us (51%)
  blocking collectives  469 us (36%)
  matrix products  113 us (9%)
  local copies, waits for them, and re-layouts  25.2 us (2%)
  between operations  14.4 us (1%)
    unnamed x10, waiting for transfers between devices  479 us
    all_gather x2, waiting for transfers between devices, apply_operator(): field_all = lax.all_gather(field_low[None], 'period', axis=0, tiled=True)  189 us
    psum x2, blocking collectives, lanczos_step(): inner_sum = lax.psum(local_mean(current * image), ('period', 'half'))  155 us
    psum x2, blocking collectives, lanczos_step(): square_sum = lax.psum(local_mean(remainder * remainder), ('period', 'half'))  146 us
    dot_general x2, matrix products, apply_operator(): jnp.einsum('pc,gkc->gpk', whole_flux, kernel_rows, precision=highest)  93.3 us
    psum x1, blocking collectives, body(): start_sum = lax.psum(local_mean(probes * probes), ('period', 'half'))  81.4 us
    all_to_all x2, blocking collectives, apply_operator(): lax.all_to_all(grouped, 'period', split_axis=0, concat_axis=0, tiled=True)  47.4 us
    all_to_all x2, blocking collectives, mix_periods(): lax.all_to_all(mixed_part, 'period', split_axis=0, concat_axis=0, tiled=T...  34.5 us
  transfers between devices with their start and end apart: 8, of which 8 were waited for; matrix products, arithmetic and copies ran while one was open for 0% of the time, Pallas kernels for 0%

commit v1 on v0

--- a/solution.py
+++ b/solution.py
@@ -111,7 +111,7 @@
         inner_sum = lax.psum(local_mean(current * image), ("period", "half"))
         alpha = inner_sum / total_rows
         remainder = image - alpha[None, :, None] * current
-        square_sum = lax.psum(local_mean(remainder * remainder), ("period", "half"))
+        square_sum = lax.psum(lax.psum(local_mean(remainder * remainder), "period"), "half")
         beta = jnp.sqrt(square_sum / total_rows + epsilon)
         return (alpha, remainder, beta)
 

time: 1310 us -> 1850 us (1.41)
  blocking collectives: 469 us -> 1020 us
    psum x2 -> x4, blocking collectives: 146 us -> 696 us  [the longest x2 579 us: lanczos_step(): lax.psum(local_mean(remainder * remainder), 'period')]
where the time goes in v1:
time: 1850 us
  blocking collectives  1020 us (55%)
  waiting for transfers between devices  667 us (36%)
  matrix products  113 us (6%)
  local copies, waits for them, and re-layouts  25.2 us (1%)
    psum x2, blocking collectives, lanczos_step(): lax.psum(local_mean(remainder * remainder), 'period')  579 us
    unnamed x10, waiting for transfers between devices  477 us
    all_gather x2, waiting for transfers between devices, apply_operator(): field_all = lax.all_gather(field_low[None], 'period', axis=0, tiled=True)  189 us
    psum x2, blocking collectives, lanczos_step(): inner_sum = lax.psum(local_mean(current * image), ('period', 'half'))  155 us
    psum x2, blocking collectives, lanczos_step(): lax.psum(lax.psum(local_mean(remainder * remainder), 'period'), 'half')  116 us
    dot_general x2, matrix products, apply_operator(): jnp.einsum('pc,gkc->gpk', whole_flux, kernel_rows, precision=highest)  93.3 us
    psum x1, blocking collectives, body(): start_sum = lax.psum(local_mean(probes * probes), ('period', 'half'))  81.4 us
    all_to_all x2, blocking collectives, apply_operator(): lax.all_to_all(grouped, 'period', split_axis=0, concat_axis=0, tiled=True)  47.4 us
  transfers between devices with their start and end apart: 8, of which 8 were waited for; matrix products, arithmetic and copies ran while one was open for 0% of the time, Pallas kernels for 0%

profile of v1, /device:TPU:1, one launch (start us, length us, event | category | flops | bytes accessed | tf_op | source)
XLA Modules:
  0.0 1853.3 jit_solution(3794682644688899739)
XLA Ops:
  7.2 1.0 multiply_reduce_fusion.3
  8.3 81.4 %psum.49 = f32[4]{0:T(128)S(1)} all-reduce(f32[4]{0:T(128)S(1)} %multiply_reduce_fusion.3), channel_id=1, replica_groups=mesh['period'=128,'half'=2] {'period','half'}, use_global_device_ids=true, to_apply=%region_1.0 | all-reduce | flops 4 | bytes 32 | tf_op jit(solution)/shard_map/psum | solution.py:118
  89.7 0.7 iota_add_fusion
  90.4 0.8 copy.24
  91.2 0.8 fusion.101
  92.0 2.5 all_gather.12
  94.9 0.8 convolution_bitcast_fusion.1
  95.7 4.4 fusion.38
  100.1 5.1 copy.26
  106.4 221.5 %all-reduce.5.cloned.1.call-done = f32[128,4,1536]{2,1,0:T(4,128)} async-done(((f32[128,4,1536]{2,1,0:T(4,128)}), f32[128,4,1536]{2,1,0:T(4,128)}) %all-reduce.5.cloned.1.call-update) | async-done | bytes 3145744
  328.0 1.4 dynamic-slice_bitcast_fusion.1
  329.4 4.9 collective-permute-start
  335.2 46.6 %fusion.32 = f32[128,4,12]{0,1,2:T(4,128)S(1)} fusion(s32[3072]{0:T(1024)S(1)} %bitcast.132, s32[128,12]{0,1:T(8,128)S(1)} %copy.23, s32[3072]{0:T(1024)S(1)} %bitcast.130, s32[128,12]{0,1:T(8,128)S(1)} %copy.22, f32[4,1536]{1,0:T(4,128)S(1)} %collective-permute-done, f32[4,1536]{1,0:T(4,128)S(1)} %dynamic-slice_bitcast_fusion.1, pred[]{:T(512)S(6)} %eq.36), kind=kOutput, calls=%fused_computation.35 | convolution fusion | flops 268996608 | bytes 110593 | tf_op jit(solution)/shard_map/pc,gkc->gpk/dot_general | solution.py:80
  382.0 23.7 %all_to_all.20 = f32[128,4,12]{2,1,0:T(4,128)S(1)} all-to-all(f32[128,4,12]{2,1,0:T(4,128)S(1)} %copy.27), channel_id=1, replica_groups=mesh['period'=128,'half'=2] {'period'}, dimensions={0} | all-to-all | bytes 49152 | tf_op jit(solution)/shard_map/all_to_all | solution.py:82
  406.4 17.2 all_to_all.21
  423.7 0.8 convert_element_type.80
  424.8 94.2 %all-gather.3.cloned.1.call-done = bf16[128,4,1536]{2,1,0:T(4,128)(2,1)} async-done(((bf16[1,4,1536]{2,1,0:T(4,128)(2,1)}), bf16[128,4,1536]{2,1,0:T(4,128)(2,1)}) %all-gather.3.cloned.1.call-update) | async-done | bytes 1572880 | tf_op jit(solution)/shard_map/all_gather | solution.py:89
  519.0 2.0 fusion.24
  521.7 0.6 fusion.16
  523.0 0.7 copy.52
  523.7 1.3 reshape.130
  525.1 16.9 reduce-scatter.7.cloned.1.call-done
  542.0 1.2 reshape.131
  543.7 77.4 %psum.50 = f32[4]{0:T(128)S(1)} all-reduce(f32[4]{0:T(128)S(1)} %fusion.68), channel_id=1, replica_groups=mesh['period'=128,'half'=2] {'period','half'}, use_global_device_ids=true, to_apply=%region_5.6 | all-reduce | flops 4 | bytes 32 | tf_op jit(solution)/shard_map/psum | solution.py:111
  621.3 289.7 %psum.51 = f32[4]{0:T(128)S(1)} all-reduce(f32[4]{0:T(128)S(1)} %multiply_reduce_fusion.2), channel_id=1, replica_groups=mesh['period'=128,'half'=2] {'period'}, use_global_device_ids=true, to_apply=%region_7.8 | all-reduce | flops 4 | bytes 32 | tf_op jit(solution)/shard_map/psum | solution.py:114
  911.0 58.2 %psum.52 = f32[4]{0:T(128)S(1)} all-reduce(f32[4]{0:T(128)S(1)} %psum.51), channel_id=1, replica_groups=mesh['period'=128,'half'=2] {'half'}, use_global_device_ids=true, to_apply=%region_8.9 | all-reduce | flops 4 | bytes 32 | tf_op jit(solution)/shard_map/psum | solution.py:114
  969.3 1.9 all_gather.14
  971.6 0.8 convolution_bitcast_fusion
  972.4 4.4 fusion.36
  976.7 5.1 copy.34
  981.9 222.0 %all-reduce.7.cloned.1.call-done = f32[128,4,1536]{2,1,0:T(4,128)} async-done(((f32[128,4,1536]{2,1,0:T(4,128)}), f32[128,4,1536]{2,1,0:T(4,128)}) %all-reduce.7.cloned.1.call-update) | async-done | bytes 3145744
  1204.0 1.4 dynamic-slice_bitcast_fusion
  1205.3 4.9 collective-permute-start.1
  1210.3 0.8 collective-permute-done.1
  1211.1 46.6 %fusion.33 = f32[128,4,12]{0,1,2:T(4,128)S(1)} fusion(s32[3072]{0:T(1024)S(1)} %bitcast.133, s32[128,12]{0,1:T(8,128)S(1)} %copy.23, s32[3072]{0:T(1024)S(1)} %bitcast.131, s32[128,12]{0,1:T(8,128)S(1)} %copy.22, f32[4,1536]{1,0:T(4,128)S(1)} %collective-permute-done.1, f32[4,1536]{1,0:T(4,128)S(1)} %dynamic-slice_bitcast_fusion, pred[]{:T(512)S(6)} %eq.36), kind=kOutput, calls=%fused_computation.36 | convolution fusion | flops 268996608 | bytes 110593 | tf_op jit(solution)/shard_map/pc,gkc->gpk/dot_general | solution.py:80
  1258.0 23.7 %all_to_all.22 = f32[128,4,12]{2,1,0:T(4,128)S(1)} all-to-all(f32[128,4,12]{2,1,0:T(4,128)S(1)} %copy.35), channel_id=1, replica_groups=mesh['period'=128,'half'=2] {'period'}, dimensions={0} | all-to-all | bytes 49152 | tf_op jit(solution)/shard_map/all_to_all | solution.py:82
  1282.4 17.2 all_to_all.23
  1299.7 0.8 convert_element_type.88
  1300.5 94.5 %all-gather.5.cloned.1.call-done = bf16[128,4,1536]{2,1,0:T(4,128)(2,1)} async-done(((bf16[1,4,1536]{2,1,0:T(4,128)(2,1)}), bf16[128,4,1536]{2,1,0:T(4,128)(2,1)}) %all-gather.5.cloned.1.call-update) | async-done | bytes 1572880 | tf_op jit(solution)/shard_map/all_gather | solution.py:89
  1395.0 2.0 fusion.27
  1399.0 0.7 copy.54
  1399.7 1.3 reshape.132
  1401.0 16.9 reduce-scatter.9.cloned.1.call-done
  1418.0 1.2 reshape.133
  1419.7 77.4 %psum.53 = f32[4]{0:T(128)S(1)} all-reduce(f32[4]{0:T(128)S(1)} %multiply_reduce_fusion.1), channel_id=1, replica_groups=mesh['period'=128,'half'=2] {'period','half'}, use_global_device_ids=true, to_apply=%region_12.13 | all-reduce | flops 4 | bytes 32 | tf_op jit(solution)/shard_map/psum | solution.py:111
  1497.1 0.8 multiply_reduce_fusion
  1497.9 289.7 %psum.54 = f32[4]{0:T(128)S(1)} all-reduce(f32[4]{0:T(128)S(1)} %get-tuple-element.4), channel_id=1, replica_groups=mesh['period'=128,'half'=2] {'period'}, use_global_device_ids=true, to_apply=%region_14.15 | all-reduce | flops 4 | bytes 32 | tf_op jit(solution)/shard_map/psum | solution.py:114
  1787.6 58.2 %psum.55 = f32[4]{0:T(128)S(1)} all-reduce(f32[4]{0:T(128)S(1)} %psum.54), channel_id=1, replica_groups=mesh['period'=128,'half'=2] {'half'}, use_global_device_ids=true, to_apply=%region_15.16 | all-reduce | flops 4 | bytes 32 | tf_op jit(solution)/shard_map/psum | solution.py:114
  (66 shorter events, 10.4 us)
Async XLA Ops:
  7.2 87.3 %copy-start = (bf16[8,512,256]{2,1,0:T(8,128)(2,1)S(1)}, bf16[8,512,256]{2,1,0:T(8,128)(2,1)}, u32[]{:S(2)}) copy-start(bf16[8,512,256]{2,1,0:T(8,128)(2,1)} %param.8) | copy-start | bytes 6291460
  7.2 88.5 %copy-start.3 = (s32[8,4]{0,1:T(4,128)S(1)}, s32[8,4]{0,1:T(4,128)}, u32[]{:S(2)}) copy-start(s32[8,4]{0,1:T(4,128)} %param.10) | copy-start | bytes 388
  7.2 320.8 %all-reduce.5.cloned.1.call-start = ((), (), s32[]{:S(2)}) async-start(), calls=%async_computation.10 | async-start | bytes 6291456
  105.2 0.7 copy-start.5
  105.2 229.1 %copy-start.2 = (s32[2,3072]{1,0:T(2,128)S(1)}, s32[2,3072]{1,0:T(2,128)}, u32[]{:S(2)}) copy-start(s32[2,3072]{1,0:T(2,128)} %param.12) | copy-start | bytes 73732
  105.2 413.8 %all-gather.3.cloned.1.call-start = ((), (), s32[]{:S(2)}) async-start(), calls=%async_computation.6 | async-start | bytes 1585152 | tf_op jit(solution)/shard_map/all_gather | solution.py:89
  329.4 5.8 collective-permute-start
  335.2 70.5 %copy-start.1 = (f32[128,128]{1,0:T(8,128)S(1)}, f32[128,128]{1,0:T(8,128)}, u32[]{:S(2)}) copy-start(f32[128,128]{1,0:T(8,128)} %param.13) | copy-start | bytes 196612
  335.2 89.6 %copy-start.4 = (f32[8,4]{0,1:T(4,128)S(1)}, f32[8,4]{0,1:T(4,128)}, u32[]{:S(2)}) copy-start(f32[8,4]{0,1:T(4,128)} %param.9) | copy-start | bytes 388
  424.5 117.5 %reduce-scatter.7.cloned.1.call-start = ((), (), s32[]{:S(2)}) async-start(), calls=%async_computation.8 | async-start | bytes 196608
  525.0 678.9 %all-reduce.7.cloned.1.call-start = ((), (), s32[]{:S(2)}) async-start(), calls=%async_computation.11 | async-start | bytes 6291456
  981.9 413.1 %all-gather.5.cloned.1.call-start = ((), (), s32[]{:S(2)}) async-start(), calls=%async_computation.7 | async-start | bytes 1585152 | tf_op jit(solution)/shard_map/all_gather | solution.py:89
  1205.3 5.8 collective-permute-start.1
  1300.5 117.5 %reduce-scatter.9.cloned.1.call-start = ((), (), s32[]{:S(2)}) async-start(), calls=%async_computation.9 | async-start | bytes 196608
Sparse Core Ops, SparseCore 0:
  105.3 222.5 all-reduce.4
  424.6 94.3 all-gather.2
  525.2 16.7 reduce-scatter.6
  982.0 221.9 all-reduce.6
  1300.6 94.3 all-gather.4
  1401.2 16.7 reduce-scatter.8
